TPU v7x, 128 devices: a whole 4x4x4 slice. The times are simulated.
128 devices in a mesh: blk: 32 (over x_hi, z, y), grp: 4 (over x_lo, core).
Axes of the slice: x: 4 (x_hi: 2, x_lo: 2; x = x_hi * 2 + x_lo), y: 4, z: 4, core: 2. Of those that a mesh axis runs over, the one named last changes fastest.
Arguments:
- images: bfloat16 [8192, 1536], P('blk'), may hold values from -100 to 100
- defocus: float32 [8192], P('blk'), may hold values from 1 to 12
- class_id: int32 [8192, 1], P('blk'), may hold values from 0 to 255; in each aligned block of 256 rows (0 to 255, 256 to 511, ...) at most 2 rows name the same one
- rotation_id: int32 [8192], P('blk'), may hold values from 0 to 31
- shift_id: int32 [8192], P('blk'), may hold values from 0 to 8
- references: float32 [4, 64, 1536], P('grp', 'blk'), may hold values from -4 to 4
- owner: int32 [4, 64], P('grp'), may hold values from 0 to 63, as said below
- inv_noise: float32 [24], replicated, may hold values from 0.5 to 2
- prior: float32 [24], replicated, may hold values from 0.5 to 2
Outputs:
- evidence: float32 [8192], P('blk')
- new_refs: float32 [4, 64, 1536], P('grp', 'blk')
Inputs may be any that keep to these rules, and one draw needn't show every extreme that they name: `class_id`: among the particles of one index of blk, no class is assigned to more than 2 particles, and some class to exactly 2. `owner`: each row is a permutation of 0 to 63.
All inputs are finite; a program needn't handle non-finite values.
Results may differ from a plain program's by a relative error of at most 0.0036.
Values sent between devices are 32-bit elements; how exact they have to be, the bound alone decides.
No kernel may reach another device: no remote copies, remote signals or barrier semaphores. Data moves between devices by JAX's collectives and lax.ppermute only.
A program may use at most 64 MiB of HBM per device.

v0:
```python
import math
import jax
import jax.numpy as jnp
from jax import lax
from jax.sharding import PartitionSpec as P

CYCLES = 24
ANGLES = 32
SHIFTS = 9
CL_DEV = 2


def contrast_table(defocus):
    frequency = (jnp.arange(CYCLES, dtype=jnp.float32) + 1.0) / CYCLES
    return -jnp.sin(defocus[:, None] * (frequency * frequency)[None, :] + 0.15)


def phase_tables():
    radius = (jnp.arange(CYCLES, dtype=jnp.float32) + 1.0) / (2.0 * CYCLES)
    bearing = 2.0 * math.pi / ANGLES * jnp.arange(ANGLES, dtype=jnp.float32)
    shift_index = jnp.arange(SHIFTS, dtype=jnp.int32)
    shift_x = (shift_index // 3 - 1).astype(jnp.float32)
    shift_y = (shift_index % 3 - 1).astype(jnp.float32)
    along = (
        shift_x[:, None] * jnp.cos(bearing)[None, :] + shift_y[:, None] * jnp.sin(bearing)[None, :]
    )
    phase = -2.0 * math.pi * radius[None, :, None] * along[:, None, :]
    return (jnp.cos(phase), jnp.sin(phase))


def weigh(images, factor):
    row_total = images.shape[0]
    grid = images.astype(jnp.float32).reshape(row_total, 2, CYCLES, ANGLES)
    return (grid * factor[:, None, :, None]).reshape(row_total, -1).astype(jnp.bfloat16)


def make_templates(ref_block):
    block_rows = ref_block.shape[0]
    grid = ref_block.reshape(block_rows, 2, CYCLES, ANGLES)
    angular = jnp.arange(ANGLES, dtype=jnp.int32)
    turning = (
        angular[:, None, None] == (angular[None, None, :] - angular[None, :, None]) % ANGLES
    ).astype(jnp.float32)
    rotated = jnp.einsum("nqka,arb->nrqkb", grid, turning, precision=lax.Precision.HIGHEST)
    phase_cos, phase_sin = phase_tables()
    rotated_re = rotated[:, :, 0][:, :, None]
    rotated_im = rotated[:, :, 1][:, :, None]
    real_part = phase_cos[None, None] * rotated_re - phase_sin[None, None] * rotated_im
    imag_part = phase_sin[None, None] * rotated_re + phase_cos[None, None] * rotated_im
    stacked = jnp.stack([real_part, imag_part], axis=3)
    return stacked.reshape(block_rows * ANGLES * SHIFTS, -1).astype(jnp.bfloat16)


def score_block(ref_block, weighted, contrast_power, score_scale):
    block_rows = ref_block.shape[0]
    templates = make_templates(ref_block)
    cross = lax.dot_general(
        templates, weighted, (((1,), (1,)), ((), ())), preferred_element_type=jnp.float32
    )
    grid = ref_block.reshape(block_rows, 2, CYCLES, ANGLES)
    power = jnp.sum(grid * grid, axis=(1, 3))
    penalty = jnp.dot(power, contrast_power.T, precision=lax.Precision.HIGHEST)
    logits = (
        cross.reshape(block_rows, ANGLES * SHIFTS, -1) - 0.5 * penalty[:, None, :]
    ) * score_scale
    return logits.reshape(block_rows * ANGLES * SHIFTS, -1)


def target_rows(relative, rotation_id, shift_id):
    inside = (relative >= 0) & (relative < CL_DEV)
    return jnp.where(inside, (relative * ANGLES + rotation_id) * SHIFTS + shift_id, -1)


def update(running, logits, target):
    peak, total, picked = running
    new_peak = jnp.maximum(peak, jnp.max(logits, axis=0))
    total = total * jnp.exp(peak - new_peak) + jnp.sum(jnp.exp(logits - new_peak[None, :]), axis=0)
    row_index = jnp.arange(logits.shape[0], dtype=jnp.int32)
    picked = picked + jnp.sum(jnp.where(row_index[:, None] == target[None, :], logits, 0.0), axis=0)
    return (new_peak, total, picked)


def align_terms(images, contrast, weight, rotation_id, shift_id):
    row_total = images.shape[0]
    phase_cos, phase_sin = phase_tables()
    chosen = (shift_id[:, None] == jnp.arange(SHIFTS, dtype=jnp.int32)[None, :]).astype(jnp.float32)
    cos_rows = jnp.dot(
        chosen, phase_cos.reshape(SHIFTS, -1), precision=lax.Precision.HIGHEST
    ).reshape(row_total, CYCLES, ANGLES)
    sin_rows = jnp.dot(
        chosen, phase_sin.reshape(SHIFTS, -1), precision=lax.Precision.HIGHEST
    ).reshape(row_total, CYCLES, ANGLES)
    grid = images.astype(jnp.float32).reshape(row_total, 2, CYCLES, ANGLES)
    unshift_re = cos_rows * grid[:, 0] + sin_rows * grid[:, 1]
    unshift_im = cos_rows * grid[:, 1] - sin_rows * grid[:, 0]
    unshifted = jnp.stack([unshift_re, unshift_im], axis=1)
    angular = jnp.arange(ANGLES, dtype=jnp.int32)
    turning = (
        angular[None, :, None] == (angular[None, None, :] + rotation_id[:, None, None]) % ANGLES
    ).astype(jnp.float32)
    aligned = jnp.einsum("pqka,pab->pqkb", unshifted, turning, precision=lax.Precision.HIGHEST)
    scaled = weight[:, None] * contrast
    numer_term = (aligned * scaled[:, None, :, None]).reshape(row_total, -1)
    denom_term = weight[:, None] * contrast * contrast
    return (numer_term, denom_term)


def finish(numerator, denominator, prior):
    grid = numerator.reshape(-1, 2, CYCLES, ANGLES)
    return (grid / (denominator + prior[None, :])[:, None, :, None]).reshape(numerator.shape)


def shards(images, defocus, class_id, rotation_id, shift_id, references, owner, inv_noise, prior):
    particle_count = images.shape[0]
    group_classes = owner.shape[1]
    class_total = group_classes * lax.axis_size("grp")
    contrast = contrast_table(defocus)
    contrast_power = contrast * contrast * inv_noise[None, :]
    weighted = weigh(images, contrast * inv_noise[None, :])
    score_scale = 1.0 / math.sqrt(images.shape[1])
    local_class = class_id[:, 0] - lax.axis_index("grp") * group_classes
    member = (local_class >= 0) & (local_class < group_classes)
    initial = (
        jnp.full((particle_count,), -1e30, jnp.float32),
        jnp.zeros((particle_count,), jnp.float32),
        jnp.zeros((particle_count,), jnp.float32),
    )
    running = initial
    shard_piece = lax.all_gather(references, "blk", axis=1, tiled=True)
    blocks = shard_piece[0].reshape(-1, CL_DEV, shard_piece.shape[2])
    firsts = CL_DEV * jnp.arange(blocks.shape[0], dtype=jnp.int32)

    def advance(running_state, entries):
        ref_block, block_first = entries
        logits = score_block(ref_block, weighted, contrast_power, score_scale)
        return (
            update(
                running_state, logits, target_rows(local_class - block_first, rotation_id, shift_id)
            ),
            None,
        )

    running, unused = lax.scan(advance, running, (blocks, firsts))
    peak, total, picked = running
    global_peak = lax.pmax(peak, "grp")
    global_total = lax.psum(total * jnp.exp(peak - global_peak), "grp")
    log_sum = global_peak + jnp.log(global_total)
    log_orients = math.log(class_total * ANGLES * SHIFTS)
    evidence = log_sum - log_orients
    weight = jnp.where(member, jnp.exp(jnp.where(member, picked - log_sum + log_orients, 0.0)), 0.0)
    numer_term, denom_term = align_terms(images, contrast, weight, rotation_id, shift_id)
    safe_class = jnp.where(member, local_class, 0)
    class_index = jnp.arange(group_classes, dtype=jnp.int32)
    slot = jnp.sum(
        jnp.where(safe_class[:, None] == class_index[None, :], owner[0][None, :], 0), axis=1
    )
    owning = (class_index[:, None] == jnp.where(member, slot, -1)[None, :]).astype(jnp.float32)
    partial_numer = jnp.dot(owning, numer_term, precision=lax.Precision.HIGHEST)
    partial_denom = jnp.dot(owning, denom_term, precision=lax.Precision.HIGHEST)
    numerator, denominator = (
        lax.psum_scatter(partial_numer, "blk", scatter_dimension=0, tiled=True),
        lax.psum_scatter(partial_denom, "blk", scatter_dimension=0, tiled=True),
    )
    new_refs = finish(numerator, denominator, prior)[None]
    return (evidence, new_refs)


def solution(mesh):
    in_specs = (
        P("blk", None),
        P("blk"),
        P("blk", None),
        P("blk"),
        P("blk"),
        P("grp", "blk", None),
        P("grp", None),
        P(),
        P(),
    )
    out_specs = (P("blk"), P("grp", "blk", None))
    return jax.shard_map(shards, mesh=mesh, in_specs=in_specs, out_specs=out_specs, check_vma=False)
```

profile of v0, /device:TPU:6, one launch (start us, length us, event | category | flops | bytes accessed | tf_op | source)
XLA Modules:
  0.0 1281.5 jit_solution(13221657645334171205)
XLA Ops:
  10.8 96.7 %all_gather.3 = f32[1,64,1536]{2,0,1:T(1,128)S(1)} all-gather(f32[1,2,1536]{2,0,1:T(1,128)S(1)} %copy.46), channel_id=1, replica_groups=mesh['blk'=32,'grp'=4] {'blk'}, dimensions={1}, use_global_device_ids=true | all-gather | bytes 405504 | tf_op jit(solution)/shard_map/all_gather | solution.py:129
  113.6 786.5 %while.18 = (s32[]{:T(128)}, f32[256]{0:T(256)S(1)}, f32[256]{0:T(256)}, f32[256]{0:T(256)}, f32[32,2,1536]{2,1,0:T(2,128)S(1)}, /*index=5*/bf16[256,1536]{1,0:T...) while((s32[]{:T(128)}, f32[256]{0:T(256)S(1)}, ...), condition=%wide.region_5.6_spmd.clone, body=%wide.region_0.5_spmd.clone.sunk | while | flops 496573632 | bytes 14409568 | solution.py:143
  119.1 4.4 pad_maximum_fusion.3
  123.5 8.9 convert_element_type.90
  143.0 4.4 pad_maximum_fusion.3
  147.4 8.9 convert_element_type.90
  167.7 4.4 pad_maximum_fusion.3
  172.0 8.9 convert_element_type.90
  192.2 4.4 pad_maximum_fusion.3
  196.6 8.9 convert_element_type.90
  216.8 4.4 pad_maximum_fusion.3
  221.2 8.9 convert_element_type.90
  241.4 4.4 pad_maximum_fusion.3
  245.8 8.9 convert_element_type.90
  266.0 4.4 pad_maximum_fusion.3
  270.4 8.9 convert_element_type.90
  290.6 4.4 pad_maximum_fusion.3
  295.0 8.9 convert_element_type.90
  315.2 4.4 pad_maximum_fusion.3
  319.6 8.9 convert_element_type.90
  339.8 4.4 pad_maximum_fusion.3
  344.2 8.9 convert_element_type.90
  364.4 4.4 pad_maximum_fusion.3
  368.8 8.9 convert_element_type.90
  389.0 4.4 pad_maximum_fusion.3
  393.4 8.9 convert_element_type.90
  413.6 4.4 pad_maximum_fusion.3
  418.0 8.9 convert_element_type.90
  438.2 4.4 pad_maximum_fusion.3
  442.6 8.9 convert_element_type.90
  462.8 4.4 pad_maximum_fusion.3
  467.2 8.9 convert_element_type.90
  487.4 4.4 pad_maximum_fusion.3
  491.8 8.9 convert_element_type.90
  512.0 4.4 pad_maximum_fusion.3
  516.4 8.9 convert_element_type.90
  536.6 4.4 pad_maximum_fusion.3
  541.0 8.9 convert_element_type.90
  565.6 8.9 convert_element_type.90
  585.8 4.4 pad_maximum_fusion.3
  590.2 8.9 convert_element_type.90
  610.4 4.4 pad_maximum_fusion.3
  614.8 8.9 convert_element_type.90
  639.4 8.9 convert_element_type.90
  664.0 8.9 convert_element_type.90
  684.2 4.4 pad_maximum_fusion.3
  688.6 8.9 convert_element_type.90
  713.2 8.9 convert_element_type.90
  737.8 8.9 convert_element_type.90
  762.4 8.9 convert_element_type.90
  782.6 4.4 pad_maximum_fusion.3
  787.0 8.9 convert_element_type.90
  811.6 8.9 convert_element_type.90
  836.2 8.9 convert_element_type.90
  860.8 8.9 convert_element_type.90
  881.0 4.4 pad_maximum_fusion.3
  885.3 8.9 convert_element_type.90
  900.1 5.7 pmax.7
  906.5 5.9 psum.7
  918.9 5.2 copy.51
  924.1 7.6 broadcast_multiply_fusion
  931.7 5.1 copy.53
  940.7 176.2 %all-reduce.1 = f32[64,24]{1,0:T(8,128)S(1)} all-reduce(f32[64,24]{1,0:T(8,128)S(1)} %fusion.44), channel_id=3, replica_groups=mesh['blk'=32,'grp'=4] {'blk'}, use_global_device_ids=true, to_apply=%region_10.11.clone | all-reduce | flops 1536 | bytes 12288
  1117.1 156.1 %all-reduce.4.cloned.1.call-done = f32[64,1536]{1,0:T(8,128)} async-done(((f32[64,1536]{1,0:T(8,128)}), f32[64,1536]{1,0:T(8,128)}) %all-reduce.4.cloned.1.call-update) | async-done | bytes 393232
  (897 shorter events, 419.9 us)
Async XLA Ops:
  7.2 105.1 %copy-start.2 = (s32[256]{0:T(256)S(1)}, s32[256]{0:T(256)}, u32[]{:S(2)}) copy-start(s32[256]{0:T(256)} %param.14) | copy-start | bytes 3076
  7.2 105.8 %copy-start.3 = (s32[256,1]{0,1:T(1,128)S(1)}, s32[256,1]{0,1:T(1,128)}, u32[]{:S(2)}) copy-start(s32[256,1]{0,1:T(1,128)} %param.13) | copy-start | bytes 3076
  7.2 106.4 %copy-start.1 = (s32[256]{0:T(256)S(1)}, s32[256]{0:T(256)}, u32[]{:S(2)}) copy-start(s32[256]{0:T(256)} %param.15) | copy-start | bytes 3076
  7.2 1266.0 %all-reduce.4.cloned.1.call-start = ((), (), s32[]{:S(2)}) async-start(), calls=%async_computation | async-start | bytes 786432
  132.4 2.4 copy-start.6
  156.3 2.4 copy-start.6
  180.9 2.4 copy-start.6
  205.5 2.4 copy-start.6
  230.1 2.4 copy-start.6
  254.7 2.4 copy-start.6
  279.3 2.4 copy-start.6
  303.9 2.4 copy-start.6
  328.5 2.4 copy-start.6
  353.1 2.4 copy-start.6
  377.7 2.4 copy-start.6
  402.3 2.4 copy-start.6
  426.9 2.4 copy-start.6
  451.5 2.4 copy-start.6
  476.1 2.4 copy-start.6
  500.7 2.4 copy-start.6
  525.3 2.4 copy-start.6
  549.9 2.4 copy-start.6
  574.5 2.4 copy-start.6
  599.1 2.4 copy-start.6
  623.7 2.4 copy-start.6
  648.3 2.4 copy-start.6
  672.9 2.4 copy-start.6
  697.5 2.4 copy-start.6
  722.1 2.4 copy-start.6
  746.7 2.4 copy-start.6
  771.3 2.4 copy-start.6
  795.9 2.4 copy-start.6
  820.5 2.4 copy-start.6
  845.1 2.4 copy-start.6
  869.7 2.4 copy-start.6
  894.3 2.4 copy-start.6
  918.9 5.2 copy-start
  931.7 6.8 copy-start.5
  931.7 185.3 %copy-start.4 = (f32[24]{0:T(128)S(1)}, f32[24]{0:T(128)}, u32[]{:S(2)}) copy-start(f32[24]{0:T(128)} %param.19) | copy-start | bytes 292
Sparse Core Ops, SparseCore 0:
  938.6 334.5 all-reduce.3
where the time goes:
time: 1290 us; the launch traced here: 1280 us
  other arithmetic  331 us (26%)
  local copies, waits for them, and re-layouts  329 us (26%)
  blocking collectives  285 us (22%)
  matrix products  163 us (13%)
  waiting for transfers between devices  156 us (12%)
  between operations  14.9 us (1%)
    convert_element_type x32, local copies, waits for them, and re-layouts, make_templates(): stacked.reshape(block_rows * ANGLES * SHIFTS, -1).astype(jnp.bfloat16)  285 us
    unnamed x1, blocking collectives  176 us
    unnamed x2, waiting for transfers between devices  156 us
    another operation x32, other arithmetic, make_templates(): stacked = jnp.stack([real_part, imag_part], axis=3)  139 us
    all_gather x1, blocking collectives, shards(): shard_piece = lax.all_gather(references, 'blk', axis=1, tiled=True)  96.7 us
    dot_general x32, matrix products, score_block(): lax.dot_general(templates, weighted, (((1,), (1,)), ((), ())), preferred_...  76.6 us
    another operation x32, other arithmetic  65.7 us
    dot_general x32, matrix products, score_block(): penalty = jnp.dot(power, contrast_power.T, precision=lax.Precision.HIGHEST)  50.4 us
  transfers between devices with their start and end apart: 1, of which 1 were waited for; matrix products, arithmetic and copies ran while one was open for 0% of the time, Pallas kernels for 0%

commit v1 on v0

--- a/solution.py
+++ b/solution.py
@@ -126,7 +126,9 @@
         jnp.zeros((particle_count,), jnp.float32),
     )
     running = initial
-    shard_piece = lax.all_gather(references, "blk", axis=1, tiled=True)
+    shard_piece = jnp.concatenate(
+        lax.all_to_all(jnp.stack([references] * lax.axis_size("blk")), "blk", 0, 0), axis=1
+    )
     blocks = shard_piece[0].reshape(-1, CL_DEV, shard_piece.shape[2])
     firsts = CL_DEV * jnp.arange(blocks.shape[0], dtype=jnp.int32)
 

time: 1290 us -> 1190 us (0.922)
  blocking collectives: 285 us -> 193 us
  matrix products: 163 us -> 148 us
    all_gather x1 -> x0, blocking collectives: 96.7 us -> none  [shards(): shard_piece = lax.all_gather(references, 'blk', axis=1, tiled=True)]
    dot_general x32, matrix products: 76.6 us -> 61.6 us  [score_block(): lax.dot_general(templates, weighted, (((1,), (1,)), ((), ())), preferred_...]
  transfers between devices with their start and end apart: 1 -> 2, of which waited for: 1 -> 1; matrix products, arithmetic and copies ran while one was open for 0% -> 1% of each run, Pallas kernels for 0% -> 0%
where the time goes in v1:
time: 1190 us; the launch traced here: 1180 us
  local copies, waits for them, and re-layouts  329 us (28%)
  other arithmetic  327 us (27%)
  blocking collectives  193 us (16%)
  waiting for transfers between devices  157 us (13%)
  matrix products  148 us (12%)
  between operations  14.9 us (1%)
    convert_element_type x32, local copies, waits for them, and re-layouts, make_templates(): stacked.reshape(block_rows * ANGLES * SHIFTS, -1).astype(jnp.bfloat16)  285 us
    unnamed x1, blocking collectives  181 us
    unnamed x2, waiting for transfers between devices  157 us
    another operation x32, other arithmetic, make_templates(): stacked = jnp.stack([real_part, imag_part], axis=3)  139 us
    another operation x32, other arithmetic  65.7 us
    dot_general x32, matrix products, score_block(): lax.dot_general(templates, weighted, (((1,), (1,)), ((), ())), preferred_...  61.6 us
    dot_general x32, matrix products, score_block(): penalty = jnp.dot(power, contrast_power.T, precision=lax.Precision.HIGHEST)  50.4 us
    add x32, other arithmetic, update(): picked + jnp.sum(jnp.where(row_index[:, None] == target[None, :], logits,...  39.7 us
  transfers between devices with their start and end apart: 2, of which 1 were waited for; matrix products, arithmetic and copies ran while one was open for 1% of the time, Pallas kernels for 0%

profile of v1, /device:TPU:6, one launch (start us, length us, event | category | flops | bytes accessed | tf_op | source)
XLA Modules:
  0.0 1183.2 jit_solution(6022857745491484745)
XLA Ops:
  8.8 11.1 all-to-all-start
  28.3 5.4 copy.48
  36.3 770.0 %while.18 = (s32[]{:T(128)}, f32[256]{0:T(256)S(1)}, f32[256]{0:T(256)}, f32[256]{0:T(256)}, f32[32,2,1536]{2,1,0:T(2,128)S(1)}, /*index=5*/bf16[256,1536]{1,0:T...) while((s32[]{:T(128)}, f32[256]{0:T(256)S(1)}, ...), condition=%wide.region_5.6_spmd.clone, body=%wide.region_0.5_spmd.clone.sunk | while | flops 496573632 | bytes 14409568 | solution.py:145
  41.8 4.4 pad_maximum_fusion.3
  46.1 8.9 convert_element_type.90
  65.2 4.4 pad_maximum_fusion.3
  69.5 8.9 convert_element_type.90
  89.3 4.4 pad_maximum_fusion.3
  93.6 8.9 convert_element_type.90
  113.4 4.4 pad_maximum_fusion.3
  117.7 8.9 convert_element_type.90
  137.4 4.4 pad_maximum_fusion.3
  141.8 8.9 convert_element_type.90
  161.5 4.4 pad_maximum_fusion.3
  165.9 8.9 convert_element_type.90
  185.6 4.4 pad_maximum_fusion.3
  190.0 8.9 convert_element_type.90
  209.7 4.4 pad_maximum_fusion.3
  214.0 8.9 convert_element_type.90
  233.8 4.4 pad_maximum_fusion.3
  238.1 8.9 convert_element_type.90
  257.9 4.4 pad_maximum_fusion.3
  262.2 8.9 convert_element_type.90
  281.9 4.4 pad_maximum_fusion.3
  286.3 8.9 convert_element_type.90
  306.0 4.4 pad_maximum_fusion.3
  310.4 8.9 convert_element_type.90
  330.1 4.4 pad_maximum_fusion.3
  334.5 8.9 convert_element_type.90
  354.2 4.4 pad_maximum_fusion.3
  358.5 8.9 convert_element_type.90
  382.6 8.9 convert_element_type.90
  402.4 4.4 pad_maximum_fusion.3
  406.7 8.9 convert_element_type.90
  430.8 8.9 convert_element_type.90
  450.5 4.4 pad_maximum_fusion.3
  454.9 8.9 convert_element_type.90
  479.0 8.9 convert_element_type.90
  498.7 4.4 pad_maximum_fusion.3
  503.1 8.9 convert_element_type.90
  527.1 8.9 convert_element_type.90
  546.9 4.4 pad_maximum_fusion.3
  551.2 8.9 convert_element_type.90
  575.3 8.9 convert_element_type.90
  595.0 4.4 pad_maximum_fusion.3
  599.4 8.9 convert_element_type.90
  623.5 8.9 convert_element_type.90
  643.2 4.4 pad_maximum_fusion.3
  647.6 8.9 convert_element_type.90
  671.6 8.9 convert_element_type.90
  691.4 4.4 pad_maximum_fusion.3
  695.7 8.9 convert_element_type.90
  715.5 4.4 pad_maximum_fusion.3
  719.8 8.9 convert_element_type.90
  743.9 8.9 convert_element_type.90
  763.6 4.4 pad_maximum_fusion.3
  768.0 8.9 convert_element_type.90
  792.1 8.9 convert_element_type.90
  806.3 5.6 pmax.7
  812.6 6.4 psum.7
  821.2 7.6 broadcast_multiply_fusion
  828.8 5.1 copy.50
  836.6 181.3 %all-reduce.1 = f32[64,24]{1,0:T(8,128)S(1)} all-reduce(f32[64,24]{1,0:T(8,128)S(1)} %fusion.44), channel_id=3, replica_groups=mesh['blk'=32,'grp'=4] {'blk'}, use_global_device_ids=true, to_apply=%region_10.11.clone | all-reduce | flops 1536 | bytes 12288
  1018.1 156.9 %all-reduce.4.cloned.1.call-done = f32[64,1536]{1,0:T(8,128)} async-done(((f32[64,1536]{1,0:T(8,128)}), f32[64,1536]{1,0:T(8,128)}) %all-reduce.4.cloned.1.call-update) | async-done | bytes 393232
  (900 shorter events, 400.8 us)
Async XLA Ops:
  7.2 15.6 %copy-start.4 = (s32[256,1]{0,1:T(1,128)S(1)}, s32[256,1]{0,1:T(1,128)}, u32[]{:S(2)}) copy-start(s32[256,1]{0,1:T(1,128)} %param.13) | copy-start | bytes 3076
  7.2 15.6 %copy-start.5 = (s32[1,64]{1,0:T(1,128)S(1)}, s32[1,64]{1,0:T(1,128)}, u32[]{:S(2)}) copy-start(s32[1,64]{1,0:T(1,128)} %param.17) | copy-start | bytes 772
  7.2 16.3 %copy-start.1 = (s32[256]{0:T(256)S(1)}, s32[256]{0:T(256)}, u32[]{:S(2)}) copy-start(s32[256]{0:T(256)} %param.15) | copy-start | bytes 3076
  8.8 27.5 %all-to-all-start = ((f32[32,1,2,1536]{3,2,1,0:T(2,128)}), f32[32,1,2,1536]{3,2,1,0:T(2,128)S(1)}, u32[]{:S(2)}, u32[]{:S(2)}) async-start(f32[32,1,2,1536]{3,2,1,0:T(2,128)} %stack.15), calls=%async_computation | async-start | bytes 786432 | tf_op jit(solution)/shard_map/all_to_all | solution.py:130
  19.8 1155.2 %all-reduce.4.cloned.1.call-start = ((), (), s32[]{:S(2)}) async-start(), calls=%async_computation.1 | async-start | bytes 786432
  28.3 5.4 copy-start.8
  28.3 7.2 copy-start.2
  28.3 8.0 copy-start
  55.1 1.9 copy-start.7
  78.5 1.9 copy-start.7
  102.6 1.9 copy-start.7
  126.6 1.9 copy-start.7
  150.7 1.9 copy-start.7
  174.8 1.9 copy-start.7
  198.9 1.9 copy-start.7
  223.0 1.9 copy-start.7
  247.1 1.9 copy-start.7
  271.1 1.9 copy-start.7
  295.2 1.9 copy-start.7
  319.3 1.9 copy-start.7
  343.4 1.9 copy-start.7
  367.5 1.9 copy-start.7
  391.6 1.9 copy-start.7
  415.6 1.9 copy-start.7
  439.7 1.9 copy-start.7
  463.8 1.9 copy-start.7
  487.9 1.9 copy-start.7
  512.0 1.9 copy-start.7
  536.1 1.9 copy-start.7
  560.1 1.9 copy-start.7
  584.2 1.9 copy-start.7
  608.3 1.9 copy-start.7
  632.4 1.9 copy-start.7
  656.5 1.9 copy-start.7
  680.6 1.9 copy-start.7
  704.7 1.9 copy-start.7
  728.7 1.9 copy-start.7
  752.8 1.9 copy-start.7
  776.9 1.9 copy-start.7
  801.0 1.9 copy-start.7
  828.8 5.1 copy-start.3
  828.8 189.1 %copy-start.6 = (f32[24]{0:T(128)S(1)}, f32[24]{0:T(128)}, u32[]{:S(2)}) copy-start(f32[24]{0:T(128)} %param.19) | copy-start | bytes 292
Sparse Core Ops, SparseCore 0:
  835.7 339.2 all-reduce.3
